TPU v7x, 32 devices: a whole 2x2x4 slice. The times are simulated.
32 devices in a mesh: trc: 4 (over z), lat: 4 (over y, x), lon: 2 (over core).
Axes of the slice: x: 2, y: 2, z: 4, core: 2. Of those that a mesh axis runs over, the one named last changes fastest.
Arguments:
- tracers: float32 [8, 16, 128, 128], P('trc', 'lat', 'lon'), may hold values from -6 to 6
- land_mask: int32 [16, 128], P('lat', 'lon'), may hold values 0 or 1
- bottom_level: int32 [16, 128], P('lat', 'lon'), may hold values from 1 to 128
- bottom_part: float32 [16, 128], P('lat', 'lon'), may hold values from 0.05 to 1
- velocity: float32 [2, 2, 8, 32768], P(None, None, ('lat', 'lon'), 'trc'), may hold values from -0.45 to 0.45
- upwelling: float32 [2, 8, 32768], P(None, ('lat', 'lon'), 'trc'), may hold values from -0.3 to 0.3
- diffusivity: float32 [2, 8, 32768], P(None, ('lat', 'lon'), 'trc'), may hold values from 0.08 to 0.32
Outputs:
- tracers_out: float32 [8, 16, 128, 128], P('trc', 'lat', 'lon')
All inputs are finite; a program needn't handle non-finite values. No bound on the sum of `land_mask` on one device may be relied on, other than what follows from the above.
Results may differ from a plain program's by a relative error of at most 0.0003.
Values sent between devices are 32-bit elements; how exact they have to be, the bound alone decides.
A program may use at most 64 MiB of HBM per device.

v0:
```python
import jax
import jax.numpy as jnp
from jax import lax
from jax.sharding import PartitionSpec as P

STEPS = 2
fraction_floor = 0.25


def with_halo(block, sides, width):
    for axis, dim in sides:
        count = lax.axis_size(axis)
        forward = [(i, i + 1) for i in range(count - 1)]
        backward = [(target, source) for source, target in forward]
        low = lax.ppermute(
            lax.slice_in_dim(block, block.shape[dim] - width, None, axis=dim), axis, forward
        )
        high = lax.ppermute(lax.slice_in_dim(block, 0, width, axis=dim), axis, backward)
        block = jnp.concatenate([low, block, high], axis=dim)
    return block


def minmod(first, second):
    return 0.5 * (jnp.sign(first) + jnp.sign(second)) * jnp.minimum(jnp.abs(first), jnp.abs(second))


def window(array, start, stop, offset):
    return lax.slice_in_dim(array, start, stop, axis=array.ndim + offset)


def face_divergence(field, speed, mixing, fraction, offset):
    extent = field.shape[field.ndim + offset]
    before = window(field, 0, extent - 3, offset)
    lower = window(field, 1, extent - 2, offset)
    upper = window(field, 2, extent - 1, offset)
    after = window(field, 3, extent, offset)
    face_speed = 0.5 * (window(speed, 1, extent - 2, offset) + window(speed, 2, extent - 1, offset))
    face_area = jnp.minimum(
        window(fraction, 1, extent - 2, offset), window(fraction, 2, extent - 1, offset)
    )
    face_mixing = 0.5 * (
        window(mixing, 1, extent - 2, offset) + window(mixing, 2, extent - 1, offset)
    )
    jump = upper - lower
    damping = 0.5 * (1.0 - jnp.abs(face_speed))
    from_lower = lower + damping * minmod(lower - before, jump)
    from_upper = upper - damping * minmod(jump, after - upper)
    face_value = jnp.where(face_speed >= 0.0, from_lower, from_upper)
    face_flux = face_area * (face_speed * face_value - face_mixing * jump)
    return window(face_flux, 1, extent - 3, offset) - window(face_flux, 0, extent - 4, offset)


def substep(field, fraction, eastward, northward, mixing, rising):
    across_rows = face_divergence(field, northward, mixing, fraction, -3)[..., 2:-2, :]
    across_cols = face_divergence(field, eastward, mixing, fraction, -2)[..., 2:-2, :, :]
    centre = field[..., 2:-2, 2:-2, :]
    wet_share = fraction[2:-2, 2:-2, :]
    top_area = jnp.minimum(wet_share[:, :, :-1], wet_share[:, :, 1:])
    lifting = rising[:, :, :-1]
    carried = jnp.where(lifting >= 0.0, centre[..., :-1], centre[..., 1:])
    vertical = top_area * lifting * carried
    closed = jnp.zeros(vertical.shape[:-1] + (1,), jnp.float32)
    across_levels = jnp.concatenate([vertical, closed], axis=-1) - jnp.concatenate(
        [closed, vertical], axis=-1
    )
    return centre - (across_rows + across_cols + across_levels) / jnp.maximum(
        wet_share, fraction_floor
    )


def cell_fraction(land_mask, bottom_level, bottom_part, levels):
    level_index = lax.broadcasted_iota(jnp.int32, land_mask.shape + (levels,), 2)
    deepest = bottom_level[:, :, None] - 1
    full_cell = (level_index < deepest).astype(jnp.float32)
    last_cell = (level_index == deepest).astype(jnp.float32) * bottom_part[:, :, None]
    return land_mask.astype(jnp.float32)[:, :, None] * (full_cell + last_cell)


def body(tracers, land_mask, bottom_level, bottom_part, velocity, upwelling, diffusivity):
    levels = tracers.shape[3]
    block_shape = (tracers.shape[1], tracers.shape[2], levels)
    fraction = cell_fraction(land_mask, bottom_level, bottom_part, levels)
    tracer_count = tracers.shape[0]
    collected = []
    moved = (
        lax.all_gather(velocity, "trc", axis=3, tiled=True),
        lax.all_gather(upwelling, "trc", axis=2, tiled=True),
        lax.all_gather(diffusivity, "trc", axis=2, tiled=True),
    )
    speeds = moved[0].reshape((STEPS, 2) + block_shape)
    rises = moved[1].reshape((STEPS,) + block_shape)
    mixes = moved[2].reshape((STEPS,) + block_shape)
    collected = [
        (speeds[number, 0], speeds[number, 1], mixes[number], rises[number])
        for number in range(STEPS)
    ]
    field = tracers
    wide_frac = fraction
    for number in range(STEPS):
        eastward, northward, mixing, rising = collected[number]
        extras = [fraction[None]] if number == 0 else []
        stack = jnp.concatenate(
            [field] + extras + [jnp.stack([eastward, northward, mixing])], axis=0
        )
        widened = with_halo(stack, (("lat", 1), ("lon", 2)), 2)
        if number == 0:
            wide_frac = widened[tracer_count]
            moved_flows = widened[tracer_count + 1 :]
        else:
            moved_flows = widened[tracer_count:]
        field = substep(
            widened[:tracer_count],
            wide_frac,
            moved_flows[0],
            moved_flows[1],
            moved_flows[2],
            rising,
        )
    return field


def solution(mesh):
    placed = (
        P("trc", "lat", "lon", None),
        P("lat", "lon"),
        P("lat", "lon"),
        P("lat", "lon"),
        P(None, None, ("lat", "lon"), "trc"),
        P(None, ("lat", "lon"), "trc"),
        P(None, ("lat", "lon"), "trc"),
    )
    return jax.shard_map(
        body, mesh=mesh, in_specs=placed, out_specs=P("trc", "lat", "lon", None), check_vma=False
    )
```

profile of v0, /device:TPU:0, one launch (start us, length us, event | category | flops | bytes accessed | tf_op | source)
XLA Modules:
  0.0 89.0 jit_solution(9641395497896303604)
XLA Ops:
  0.0 0.7 convert_element_type.14
  0.7 0.7 broadcast_add_fusion
  1.4 15.8 %all_gather.10 = f32[2,1,32768]{2,1,0:T(1,128)S(1)} all-gather(f32[2,1,8192]{2,1,0:T(1,128)} %param.13), channel_id=1, replica_groups=mesh['trc'=4,'lat'=4,'lon'=2] {'trc'}, dimensions={2}, use_global_device_ids=true | all-gather | bytes 327680 | tf_op jit(solution)/shard_map/all_gather | solution.py:88
  17.3 16.4 %all_gather.9 = f32[2,2,1,32768]{3,2,1,0:T(1,128)S(1)} all-gather(f32[2,2,1,8192]{3,2,1,0:T(1,128)} %param.11), channel_id=1, replica_groups=mesh['trc'=4,'lat'=4,'lon'=2] {'trc'}, dimensions={3}, use_global_device_ids=true | all-gather | bytes 655360 | tf_op jit(solution)/shard_map/all_gather | solution.py:86
  34.0 3.4 %collective-permute-start = (f32[6,2,64,128]{3,2,1,0:T(8,128)S(1)}, f32[6,2,64,128]{3,2,1,0:T(8,128)S(1)}, u32[]{:S(2)}, u32[]{:S(2)}) collective-permute-start(f32[6,2,64,128]{3,2,1,0:T(8,128)S(1)} %get-tuple-element.25), channel_id=1, source_target_pairs={{0,2},{2,4},{4,6},{1,3},{3,5},{5,7},{8,10},{10,12},{12,14},{9,11},... | collective-permute-start | bytes 1179656 | tf_op jit(solution)/shard_map/ppermute | solution.py:15
  37.4 1.3 %collective-permute-start.1 = (f32[6,2,64,128]{3,2,1,0:T(8,128)S(1)}, f32[6,2,64,128]{3,2,1,0:T(8,128)S(1)}, u32[]{:S(2)}, u32[]{:S(2)}) collective-permute-start(f32[6,2,64,128]{3,2,1,0:T(8,128)S(1)} %get-tuple-element.26), channel_id=1, source_target_pairs={{2,0},{4,2},{6,4},{3,1},{5,3},{7,5},{10,8},{12,10},{14,12},{11,9},... | collective-permute-start | bytes 1179656 | tf_op jit(solution)/shard_map/ppermute | solution.py:18
  38.8 13.8 %all_gather.11 = f32[2,1,32768]{2,1,0:T(1,128)S(1)} all-gather(f32[2,1,8192]{2,1,0:T(1,128)S(1)} %copy-done.1), channel_id=1, replica_groups=mesh['trc'=4,'lat'=4,'lon'=2] {'trc'}, dimensions={2}, use_global_device_ids=true | all-gather | bytes 327680 | tf_op jit(solution)/shard_map/all_gather | solution.py:87
  52.7 1.3 %collective-permute-start.2 = (f32[6,8,2,128]{3,2,1,0:T(2,128)S(1)}, f32[6,8,2,128]{3,2,1,0:T(2,128)S(1)}, u32[]{:S(2)}, u32[]{:S(2)}) collective-permute-start(f32[6,8,2,128]{3,2,1,0:T(2,128)S(1)} %get-tuple-element.16), channel_id=1, source_target_pairs={{0,1},{2,3},{4,5},{6,7},{8,9},{10,11},{12,13},{14,15},{16,17},{18,... | collective-permute-start | bytes 147464 | tf_op jit(solution)/shard_map/ppermute | solution.py:15
  54.0 1.3 %collective-permute-start.3 = (f32[6,8,2,128]{3,2,1,0:T(2,128)S(1)}, f32[6,8,2,128]{3,2,1,0:T(2,128)S(1)}, u32[]{:S(2)}, u32[]{:S(2)}) collective-permute-start(f32[6,8,2,128]{3,2,1,0:T(2,128)S(1)} %get-tuple-element.17), channel_id=1, source_target_pairs={{1,0},{3,2},{5,4},{7,6},{9,8},{11,10},{13,12},{15,14},{17,16},{19,... | collective-permute-start | bytes 147464 | tf_op jit(solution)/shard_map/ppermute | solution.py:18
  55.3 1.8 %collective-permute-done.3 = f32[6,8,2,128]{3,2,1,0:T(2,128)S(1)} collective-permute-done((f32[6,8,2,128]{3,2,1,0:T(2,128)S(1)}, f32[6,8,2,128]{3,2,1,0:T(2,128)S(1)}, u32[]{:S(2)}, u32[]{:S(2)}) %collective-permute-start.3) | collective-permute-done | bytes 49184 | tf_op jit(solution)/shard_map/ppermute | solution.py:18
  57.1 0.2 pad_maximum_fusion
  57.8 0.3 subtract_multiply_fusion.3
  58.3 1.0 %subtract_multiply_fusion.1 = f32[2,8,65,128]{3,2,1,0:T(8,128)S(1)} fusion(f32[6,8,2,128]{3,2,1,0:T(2,128)S(1)} %collective-permute-done.3, f32[6,2,64,128]{3,2,1,0:T(8,128)S(1)} %collective-permute-done.1, f32[6,4,64,128]{3,2,1,0:T(8,128)S(1)} %constant_dynamic-update-slice_fusion, f32[6,2,64,128]{3,2,1,0:T(8,128)S(1)} %collective-permute-done, ...), kind=kLoop, calls=%fused_computation.33 | loop fusion | flops 5058560 | bytes 3335168 | tf_op jit(solution)/shard_map/mul | solution.py:49
  59.6 0.2 fusion.24
  59.9 4.6 %collective-permute-start.4 = (f32[5,2,64,128]{3,2,1,0:T(8,128)S(1)}, f32[5,2,64,128]{3,2,1,0:T(8,128)S(1)}, u32[]{:S(2)}, u32[]{:S(2)}) collective-permute-start(f32[5,2,64,128]{3,2,1,0:T(8,128)S(1)} %get-tuple-element.27), channel_id=1, source_target_pairs={{0,2},{2,4},{4,6},{1,3},{3,5},{5,7},{8,10},{10,12},{12,14},{9,11},... | collective-permute-start | bytes 983048 | tf_op jit(solution)/shard_map/ppermute | solution.py:15
  64.5 1.3 %collective-permute-start.5 = (f32[5,2,64,128]{3,2,1,0:T(8,128)S(1)}, f32[5,2,64,128]{3,2,1,0:T(8,128)S(1)}, u32[]{:S(2)}, u32[]{:S(2)}) collective-permute-start(f32[5,2,64,128]{3,2,1,0:T(8,128)S(1)} %get-tuple-element.28), channel_id=1, source_target_pairs={{2,0},{4,2},{6,4},{3,1},{5,3},{7,5},{10,8},{12,10},{14,12},{11,9},... | collective-permute-start | bytes 983048 | tf_op jit(solution)/shard_map/ppermute | solution.py:18
  65.8 5.9 %collective-permute-done.4 = f32[5,2,64,128]{3,2,1,0:T(8,128)S(1)} collective-permute-done((f32[5,2,64,128]{3,2,1,0:T(8,128)S(1)}, f32[5,2,64,128]{3,2,1,0:T(8,128)S(1)}, u32[]{:S(2)}, u32[]{:S(2)}) %collective-permute-start.4) | collective-permute-done | bytes 327712 | tf_op jit(solution)/shard_map/ppermute | solution.py:15
  71.7 9.8 %collective-permute-done.5 = f32[5,2,64,128]{3,2,1,0:T(8,128)S(1)} collective-permute-done((f32[5,2,64,128]{3,2,1,0:T(8,128)S(1)}, f32[5,2,64,128]{3,2,1,0:T(8,128)S(1)}, u32[]{:S(2)}, u32[]{:S(2)}) %collective-permute-start.5) | collective-permute-done | bytes 327712 | tf_op jit(solution)/shard_map/ppermute | solution.py:18
  81.6 1.3 %collective-permute-start.6 = (f32[5,8,2,128]{3,2,1,0:T(2,128)S(1)}, f32[5,8,2,128]{3,2,1,0:T(2,128)S(1)}, u32[]{:S(2)}, u32[]{:S(2)}) collective-permute-start(f32[5,8,2,128]{3,2,1,0:T(2,128)S(1)} %get-tuple-element.23), channel_id=1, source_target_pairs={{0,1},{2,3},{4,5},{6,7},{8,9},{10,11},{12,13},{14,15},{16,17},{18,... | collective-permute-start | bytes 122888 | tf_op jit(solution)/shard_map/ppermute | solution.py:15
  82.9 1.3 %collective-permute-start.7 = (f32[5,8,2,128]{3,2,1,0:T(2,128)S(1)}, f32[5,8,2,128]{3,2,1,0:T(2,128)S(1)}, u32[]{:S(2)}, u32[]{:S(2)}) collective-permute-start(f32[5,8,2,128]{3,2,1,0:T(2,128)S(1)} %get-tuple-element.24), channel_id=1, source_target_pairs={{1,0},{3,2},{5,4},{7,6},{9,8},{11,10},{13,12},{15,14},{17,16},{19,... | collective-permute-start | bytes 122888 | tf_op jit(solution)/shard_map/ppermute | solution.py:18
  84.3 1.7 %collective-permute-done.7 = f32[5,8,2,128]{3,2,1,0:T(2,128)S(1)} collective-permute-done((f32[5,8,2,128]{3,2,1,0:T(2,128)S(1)}, f32[5,8,2,128]{3,2,1,0:T(2,128)S(1)}, u32[]{:S(2)}, u32[]{:S(2)}) %collective-permute-start.7) | collective-permute-done | bytes 40992 | tf_op jit(solution)/shard_map/ppermute | solution.py:18
  86.5 0.3 subtract_multiply_fusion.2
  87.0 1.0 %subtract_multiply_fusion = f32[2,8,65,128]{3,2,1,0:T(8,128)S(1)} fusion(f32[5,8,2,128]{3,2,1,0:T(2,128)S(1)} %collective-permute-done.7, f32[5,2,64,128]{3,2,1,0:T(8,128)S(1)} %collective-permute-done.5, f32[1,4,64,128]{3,2,1,0:T(8,128)S(1)} %bitcast.48, f32[1,4,64,128]{3,2,1,0:T(8,128)S(1)} %get-tuple-element.34, ...), kind=kLoop, calls=%fused_computation.29 | loop fusion | flops 6656000 | bytes 3056640 | tf_op jit(solution)/shard_map/mul | solution.py:49
  88.1 0.9 %fusion.20 = f32[2,4,64,128]{3,2,1,0:T(8,128)} fusion(f32[2,4,64,128]{3,2,1,0:T(8,128)S(1)} %fusion.24, f32[2,8,64,128]{3,2,1,0:T(8,128)S(1)} %get-tuple-element.30, f32[2,8,64,128]{3,2,1,0:T(8,128)S(1)} %get-tuple-element.29, f32[2,4,68,128]{3,2,1,0:T(8,128)S(1)} %get-tuple-element.36, f32[2,4,68,128]{3,2,1,0:T(8,128)S(1)} %get-tuple-element.35, ...), kind=kLoop, calls=%fused_computation.70 | loop fusion | flops 458752 | bytes 1964032 | tf_op jit(solution)/shard_map/sub | solution.py:66
  (46 shorter events, 2.1 us)
Async XLA Ops:
  0.0 33.7 %copy-start = (f32[2,4,64,128]{3,2,1,0:T(8,128)S(1)}, f32[2,4,64,128]{3,2,1,0:T(8,128)}, u32[]{:S(2)}) copy-start(f32[2,4,64,128]{3,2,1,0:T(8,128)} %param.7) | copy-start | bytes 786436
  0.0 33.7 %copy-start.2 = (f32[4,64]{1,0:T(4,128)S(1)}, f32[4,64]{1,0:T(4,128)}, u32[]{:S(2)}) copy-start(f32[4,64]{1,0:T(4,128)} %param.10) | copy-start | bytes 3076
  33.7 5.1 %copy-start.1 = (f32[2,1,8192]{2,1,0:T(1,128)S(1)}, f32[2,1,8192]{2,1,0:T(1,128)}, u32[]{:S(2)}) copy-start(f32[2,1,8192]{2,1,0:T(1,128)} %param.12) | copy-start | bytes 196612
  34.0 18.6 %collective-permute-start = (f32[6,2,64,128]{3,2,1,0:T(8,128)S(1)}, f32[6,2,64,128]{3,2,1,0:T(8,128)S(1)}, u32[]{:S(2)}, u32[]{:S(2)}) collective-permute-start(f32[6,2,64,128]{3,2,1,0:T(8,128)S(1)} %get-tuple-element.25), channel_id=1, source_target_pairs={{0,2},{2,4},{4,6},{1,3},{3,5},{5,7},{8,10},{10,12},{12,14},{9,11},... | collective-permute-start | bytes 1179656 | tf_op jit(solution)/shard_map/ppermute | solution.py:15
  37.4 15.2 %collective-permute-start.1 = (f32[6,2,64,128]{3,2,1,0:T(8,128)S(1)}, f32[6,2,64,128]{3,2,1,0:T(8,128)S(1)}, u32[]{:S(2)}, u32[]{:S(2)}) collective-permute-start(f32[6,2,64,128]{3,2,1,0:T(8,128)S(1)} %get-tuple-element.26), channel_id=1, source_target_pairs={{2,0},{4,2},{6,4},{3,1},{5,3},{7,5},{10,8},{12,10},{14,12},{11,9},... | collective-permute-start | bytes 1179656 | tf_op jit(solution)/shard_map/ppermute | solution.py:18
  52.7 2.6 %collective-permute-start.2 = (f32[6,8,2,128]{3,2,1,0:T(2,128)S(1)}, f32[6,8,2,128]{3,2,1,0:T(2,128)S(1)}, u32[]{:S(2)}, u32[]{:S(2)}) collective-permute-start(f32[6,8,2,128]{3,2,1,0:T(2,128)S(1)} %get-tuple-element.16), channel_id=1, source_target_pairs={{0,1},{2,3},{4,5},{6,7},{8,9},{10,11},{12,13},{14,15},{16,17},{18,... | collective-permute-start | bytes 147464 | tf_op jit(solution)/shard_map/ppermute | solution.py:15
  54.0 3.1 %collective-permute-start.3 = (f32[6,8,2,128]{3,2,1,0:T(2,128)S(1)}, f32[6,8,2,128]{3,2,1,0:T(2,128)S(1)}, u32[]{:S(2)}, u32[]{:S(2)}) collective-permute-start(f32[6,8,2,128]{3,2,1,0:T(2,128)S(1)} %get-tuple-element.17), channel_id=1, source_target_pairs={{1,0},{3,2},{5,4},{7,6},{9,8},{11,10},{13,12},{15,14},{17,16},{19,... | collective-permute-start | bytes 147464 | tf_op jit(solution)/shard_map/ppermute | solution.py:18
  59.9 11.8 %collective-permute-start.4 = (f32[5,2,64,128]{3,2,1,0:T(8,128)S(1)}, f32[5,2,64,128]{3,2,1,0:T(8,128)S(1)}, u32[]{:S(2)}, u32[]{:S(2)}) collective-permute-start(f32[5,2,64,128]{3,2,1,0:T(8,128)S(1)} %get-tuple-element.27), channel_id=1, source_target_pairs={{0,2},{2,4},{4,6},{1,3},{3,5},{5,7},{8,10},{10,12},{12,14},{9,11},... | collective-permute-start | bytes 983048 | tf_op jit(solution)/shard_map/ppermute | solution.py:15
  64.5 17.1 %collective-permute-start.5 = (f32[5,2,64,128]{3,2,1,0:T(8,128)S(1)}, f32[5,2,64,128]{3,2,1,0:T(8,128)S(1)}, u32[]{:S(2)}, u32[]{:S(2)}) collective-permute-start(f32[5,2,64,128]{3,2,1,0:T(8,128)S(1)} %get-tuple-element.28), channel_id=1, source_target_pairs={{2,0},{4,2},{6,4},{3,1},{5,3},{7,5},{10,8},{12,10},{14,12},{11,9},... | collective-permute-start | bytes 983048 | tf_op jit(solution)/shard_map/ppermute | solution.py:18
  81.6 2.7 %collective-permute-start.6 = (f32[5,8,2,128]{3,2,1,0:T(2,128)S(1)}, f32[5,8,2,128]{3,2,1,0:T(2,128)S(1)}, u32[]{:S(2)}, u32[]{:S(2)}) collective-permute-start(f32[5,8,2,128]{3,2,1,0:T(2,128)S(1)} %get-tuple-element.23), channel_id=1, source_target_pairs={{0,1},{2,3},{4,5},{6,7},{8,9},{10,11},{12,13},{14,15},{16,17},{18,... | collective-permute-start | bytes 122888 | tf_op jit(solution)/shard_map/ppermute | solution.py:15
  82.9 3.1 %collective-permute-start.7 = (f32[5,8,2,128]{3,2,1,0:T(2,128)S(1)}, f32[5,8,2,128]{3,2,1,0:T(2,128)S(1)}, u32[]{:S(2)}, u32[]{:S(2)}) collective-permute-start(f32[5,8,2,128]{3,2,1,0:T(2,128)S(1)} %get-tuple-element.24), channel_id=1, source_target_pairs={{1,0},{3,2},{5,4},{7,6},{9,8},{11,10},{13,12},{15,14},{17,16},{19,... | collective-permute-start | bytes 122888 | tf_op jit(solution)/shard_map/ppermute | solution.py:18
where the time goes:
time: 89.3 us; the launch traced here: 89 us
  blocking collectives  46 us (52%)
  waiting for transfers between devices  19.2 us (22%)
  starting transfers between devices  15.7 us (18%)
  other arithmetic  6.98 us (8%)
    all_gather x1, blocking collectives, body(): lax.all_gather(velocity, 'trc', axis=3, tiled=True)  16.4 us
    all_gather x1, blocking collectives, body(): lax.all_gather(diffusivity, 'trc', axis=2, tiled=True)  15.8 us
    all_gather x1, blocking collectives, body(): lax.all_gather(upwelling, 'trc', axis=2, tiled=True)  13.8 us
    ppermute x4, waiting for transfers between devices, with_halo(): lax.ppermute(lax.slice_in_dim(block, 0, width, axis=dim), axis, backward)  13.3 us
    ppermute x4, starting transfers between devices, with_halo(): lax.ppermute(lax.slice_in_dim(block, block.shape[dim] - width, None, axis...  10.6 us
    ppermute x4, waiting for transfers between devices, with_halo(): lax.ppermute(lax.slice_in_dim(block, block.shape[dim] - width, None, axis...  5.93 us
    ppermute x4, starting transfers between devices, with_halo(): lax.ppermute(lax.slice_in_dim(block, 0, width, axis=dim), axis, backward)  5.17 us
    mul x6, other arithmetic, face_divergence(): face_flux = face_area * (face_speed * face_value - face_mixing * jump)  2.82 us
  transfers between devices with their start and end apart: 8, of which 4 were waited for; matrix products, arithmetic and copies ran while one was open for 0% of the time, Pallas kernels for 0%

commit v1 on v0

--- a/solution.py
+++ b/solution.py
@@ -5,6 +5,22 @@
 
 STEPS = 2
 fraction_floor = 0.25
+
+
+def gather_around(x, axis, dim):
+    ways, here, step = (lax.axis_size(axis), lax.axis_index(axis), x.shape[dim])
+    shape = [n * ways if d == dim else n for d, n in enumerate(x.shape)]
+    full = lax.dynamic_update_slice_in_dim(jnp.zeros(shape, x.dtype), x, here * step, axis=dim)
+    going_up = going_down = x
+    for far in range(1, ways // 2 + 1):
+        going_up = lax.ppermute(going_up, axis, [(d, (d + 1) % ways) for d in range(ways)])
+        full = lax.dynamic_update_slice_in_dim(full, going_up, (here - far) % ways * step, axis=dim)
+        if 2 * far < ways:
+            going_down = lax.ppermute(going_down, axis, [(d, (d - 1) % ways) for d in range(ways)])
+            full = lax.dynamic_update_slice_in_dim(
+                full, going_down, (here + far) % ways * step, axis=dim
+            )
+    return full
 
 
 def with_halo(block, sides, width):
@@ -83,7 +99,7 @@
     tracer_count = tracers.shape[0]
     collected = []
     moved = (
-        lax.all_gather(velocity, "trc", axis=3, tiled=True),
+        gather_around(velocity, "trc", 3),
         lax.all_gather(upwelling, "trc", axis=2, tiled=True),
         lax.all_gather(diffusivity, "trc", axis=2, tiled=True),
     )

time: 89.3 us -> 95.7 us (1.072)
  blocking collectives: 46 us -> 29.3 us
  waiting for transfers between devices: 19.2 us -> 33.6 us
  starting transfers between devices: 15.7 us -> 21.4 us
  local copies, waits for them, and re-layouts: 0.57 us -> 3.43 us
    all_gather x1 -> x0, blocking collectives: 16.4 us -> none  [body(): lax.all_gather(velocity, 'trc', axis=3, tiled=True)]
    ppermute x0 -> x3, starting transfers between devices: none -> 6.6 us  [the longest x1 5.1 us: gather_around(): lax.ppermute(going_down, axis, [(d, (d - 1) % ways) for d in range(ways)])]
    ppermute x4, waiting for transfers between devices: 13.3 us -> 18.8 us  [with_halo(): lax.ppermute(lax.slice_in_dim(block, 0, width, axis=dim), axis, backward)]
    ppermute x0 -> x3, waiting for transfers between devices: none -> 5.04 us  [the longest x2 5.04 us: gather_around(): lax.ppermute(going_up, axis, [(d, (d + 1) % ways) for d in range(ways)])]
    ppermute x4, waiting for transfers between devices: 5.93 us -> 9.83 us  [with_halo(): lax.ppermute(lax.slice_in_dim(block, block.shape[dim] - width, None, axis...]
    unnamed x9 -> x11, local copies, waits for them, and re-layouts: 0.05 us -> 1.85 us
    all_gather x1, blocking collectives: 15.8 us -> 14.4 us  [body(): lax.all_gather(diffusivity, 'trc', axis=2, tiled=True)]
    all_gather x1, blocking collectives: 13.8 us -> 14.9 us  [body(): lax.all_gather(upwelling, 'trc', axis=2, tiled=True)]
  transfers between devices with their start and end apart: 8 -> 11, of which waited for: 4 -> 7; matrix products, arithmetic and copies ran while one was open for 0% -> 3% of each run, Pallas kernels for 0% -> 0%
where the time goes in v1:
time: 95.7 us; the launch traced here: 95.3 us
  waiting for transfers between devices  33.6 us (35%)
  blocking collectives  29.3 us (31%)
  starting transfers between devices  21.4 us (22%)
  other arithmetic  6.95 us (7%)
  local copies, waits for them, and re-layouts  3.43 us (4%)
    ppermute x4, waiting for transfers between devices, with_halo(): lax.ppermute(lax.slice_in_dim(block, 0, width, axis=dim), axis, backward)  18.8 us
    all_gather x1, blocking collectives, body(): lax.all_gather(upwelling, 'trc', axis=2, tiled=True)  14.9 us
    all_gather x1, blocking collectives, body(): lax.all_gather(diffusivity, 'trc', axis=2, tiled=True)  14.4 us
    ppermute x4, waiting for transfers between devices, with_halo(): lax.ppermute(lax.slice_in_dim(block, block.shape[dim] - width, None, axis...  9.83 us
    ppermute x4, starting transfers between devices, with_halo(): lax.ppermute(lax.slice_in_dim(block, block.shape[dim] - width, None, axis...  9.68 us
    ppermute x4, starting transfers between devices, with_halo(): lax.ppermute(lax.slice_in_dim(block, 0, width, axis=dim), axis, backward)  5.17 us
    ppermute x1, starting transfers between devices, gather_around(): lax.ppermute(going_down, axis, [(d, (d - 1) % ways) for d in range(ways)])  5.1 us
    ppermute x2, waiting for transfers between devices, gather_around(): lax.ppermute(going_up, axis, [(d, (d + 1) % ways) for d in range(ways)])  5.04 us
  transfers between devices with their start and end apart: 11, of which 7 were waited for; matrix products, arithmetic and copies ran while one was open for 3% of the time, Pallas kernels for 0%

profile of v1, /device:TPU:0, one launch (start us, length us, event | category | flops | bytes accessed | tf_op | source)
XLA Modules:
  0.0 95.3 jit_solution(10690436065592188077)
XLA Ops:
  0.0 5.1 %collective-permute-start.1 = (f32[2,2,1,8192]{3,2,1,0:T(1,128)}, f32[2,2,1,8192]{3,2,1,0:T(1,128)S(1)}, u32[]{:S(2)}, u32[]{:S(2)}) collective-permute-start(f32[2,2,1,8192]{3,2,1,0:T(1,128)} %param.11), channel_id=1, source_target_pairs={{0,24},{8,0},{16,8},{24,16},{1,25},{9,1},{17,9},{25,17},{2,26},{10... | collective-permute-start | bytes 393224 | tf_op jit(solution)/shard_map/ppermute | solution.py:19
  6.5 14.4 %all_gather.6 = f32[2,1,32768]{2,1,0:T(1,128)S(1)} all-gather(f32[2,1,8192]{2,1,0:T(1,128)} %param.13), channel_id=1, replica_groups=mesh['trc'=4,'lat'=4,'lon'=2] {'trc'}, dimensions={2}, use_global_device_ids=true | all-gather | bytes 327680 | tf_op jit(solution)/shard_map/all_gather | solution.py:104
  20.9 1.0 %constant_dynamic-update-slice_fusion.1 = f32[6,4,64,128]{3,2,1,0:T(8,128)S(1)} fusion(f32[2,4,64,128]{3,2,1,0:T(8,128)} %param.7), kind=kLoop, calls=%fused_computation.126 | loop fusion | bytes 524288
  22.4 14.9 %all_gather.7 = f32[2,1,32768]{2,1,0:T(1,128)S(1)} all-gather(f32[2,1,8192]{2,1,0:T(1,128)S(1)} %copy-done.2), channel_id=1, replica_groups=mesh['trc'=4,'lat'=4,'lon'=2] {'trc'}, dimensions={2}, use_global_device_ids=true | all-gather | bytes 327680 | tf_op jit(solution)/shard_map/all_gather | solution.py:103
  37.3 1.5 %collective-permute-start.2 = (f32[2,2,1,8192]{3,2,1,0:T(1,128)S(1)}, f32[2,2,1,8192]{3,2,1,0:T(1,128)S(1)}, u32[]{:S(2)}, u32[]{:S(2)}) collective-permute-start(f32[2,2,1,8192]{3,2,1,0:T(1,128)S(1)} %collective-permute-done), channel_id=1, source_target_pairs={{0,8},{8,16},{16,24},{24,0},{1,9},{9,17},{17,25},{25,1},{2,10},{10... | collective-permute-start | bytes 393224 | tf_op jit(solution)/shard_map/ppermute | solution.py:16
  39.0 5.0 %collective-permute-done.2 = f32[2,2,1,8192]{3,2,1,0:T(1,128)S(1)} collective-permute-done((f32[2,2,1,8192]{3,2,1,0:T(1,128)S(1)}, f32[2,2,1,8192]{3,2,1,0:T(1,128)S(1)}, u32[]{:S(2)}, u32[]{:S(2)}) %collective-permute-start.2) | collective-permute-done | bytes 131104 | tf_op jit(solution)/shard_map/ppermute | solution.py:16
  44.8 3.4 %collective-permute-start.3 = (f32[6,2,64,128]{3,2,1,0:T(8,128)S(1)}, f32[6,2,64,128]{3,2,1,0:T(8,128)S(1)}, u32[]{:S(2)}, u32[]{:S(2)}) collective-permute-start(f32[6,2,64,128]{3,2,1,0:T(8,128)S(1)} %get-tuple-element.25), channel_id=1, source_target_pairs={{0,2},{2,4},{4,6},{1,3},{3,5},{5,7},{8,10},{10,12},{12,14},{9,11},... | collective-permute-start | bytes 1179656 | tf_op jit(solution)/shard_map/ppermute | solution.py:31
  48.2 1.3 %collective-permute-start.4 = (f32[6,2,64,128]{3,2,1,0:T(8,128)S(1)}, f32[6,2,64,128]{3,2,1,0:T(8,128)S(1)}, u32[]{:S(2)}, u32[]{:S(2)}) collective-permute-start(f32[6,2,64,128]{3,2,1,0:T(8,128)S(1)} %get-tuple-element.26), channel_id=1, source_target_pairs={{2,0},{4,2},{6,4},{3,1},{5,3},{7,5},{10,8},{12,10},{14,12},{11,9},... | collective-permute-start | bytes 1179656 | tf_op jit(solution)/shard_map/ppermute | solution.py:34
  49.6 3.9 %collective-permute-done.3 = f32[6,2,64,128]{3,2,1,0:T(8,128)S(1)} collective-permute-done((f32[6,2,64,128]{3,2,1,0:T(8,128)S(1)}, f32[6,2,64,128]{3,2,1,0:T(8,128)S(1)}, u32[]{:S(2)}, u32[]{:S(2)}) %collective-permute-start.3) | collective-permute-done | bytes 393248 | tf_op jit(solution)/shard_map/ppermute | solution.py:31
  53.5 7.6 %collective-permute-done.4 = f32[6,2,64,128]{3,2,1,0:T(8,128)S(1)} collective-permute-done((f32[6,2,64,128]{3,2,1,0:T(8,128)S(1)}, f32[6,2,64,128]{3,2,1,0:T(8,128)S(1)}, u32[]{:S(2)}, u32[]{:S(2)}) %collective-permute-start.4) | collective-permute-done | bytes 393248 | tf_op jit(solution)/shard_map/ppermute | solution.py:34
  61.1 1.3 %collective-permute-start.5 = (f32[6,8,2,128]{3,2,1,0:T(2,128)S(1)}, f32[6,8,2,128]{3,2,1,0:T(2,128)S(1)}, u32[]{:S(2)}, u32[]{:S(2)}) collective-permute-start(f32[6,8,2,128]{3,2,1,0:T(2,128)S(1)} %get-tuple-element.16), channel_id=1, source_target_pairs={{0,1},{2,3},{4,5},{6,7},{8,9},{10,11},{12,13},{14,15},{16,17},{18,... | collective-permute-start | bytes 147464 | tf_op jit(solution)/shard_map/ppermute | solution.py:31
  62.4 1.3 %collective-permute-start.6 = (f32[6,8,2,128]{3,2,1,0:T(2,128)S(1)}, f32[6,8,2,128]{3,2,1,0:T(2,128)S(1)}, u32[]{:S(2)}, u32[]{:S(2)}) collective-permute-start(f32[6,8,2,128]{3,2,1,0:T(2,128)S(1)} %get-tuple-element.17), channel_id=1, source_target_pairs={{1,0},{3,2},{5,4},{7,6},{9,8},{11,10},{13,12},{15,14},{17,16},{19,... | collective-permute-start | bytes 147464 | tf_op jit(solution)/shard_map/ppermute | solution.py:34
  63.7 1.8 %collective-permute-done.6 = f32[6,8,2,128]{3,2,1,0:T(2,128)S(1)} collective-permute-done((f32[6,8,2,128]{3,2,1,0:T(2,128)S(1)}, f32[6,8,2,128]{3,2,1,0:T(2,128)S(1)}, u32[]{:S(2)}, u32[]{:S(2)}) %collective-permute-start.6) | collective-permute-done | bytes 49184 | tf_op jit(solution)/shard_map/ppermute | solution.py:34
  66.7 1.0 %subtract_multiply_fusion.1 = f32[2,8,65,128]{3,2,1,0:T(8,128)S(1)} fusion(f32[6,8,2,128]{3,2,1,0:T(2,128)S(1)} %collective-permute-done.6, f32[6,2,64,128]{3,2,1,0:T(8,128)S(1)} %collective-permute-done.4, f32[6,4,64,128]{3,2,1,0:T(8,128)S(1)} %constant_dynamic-update-slice_fusion, f32[6,2,64,128]{3,2,1,0:T(8,128)S(1)} %collective-permute-done.3, ...), kind=kLoop, calls=%fused_computation.33 | loop fusion | flops 5058560 | bytes 3335168 | tf_op jit(solution)/shard_map/mul | solution.py:65
  67.9 0.8 copy-done
  69.2 3.4 %collective-permute-start.7 = (f32[5,2,64,128]{3,2,1,0:T(8,128)S(1)}, f32[5,2,64,128]{3,2,1,0:T(8,128)S(1)}, u32[]{:S(2)}, u32[]{:S(2)}) collective-permute-start(f32[5,2,64,128]{3,2,1,0:T(8,128)S(1)} %get-tuple-element.27), channel_id=1, source_target_pairs={{0,2},{2,4},{4,6},{1,3},{3,5},{5,7},{8,10},{10,12},{12,14},{9,11},... | collective-permute-start | bytes 983048 | tf_op jit(solution)/shard_map/ppermute | solution.py:31
  72.6 1.3 %collective-permute-start.8 = (f32[5,2,64,128]{3,2,1,0:T(8,128)S(1)}, f32[5,2,64,128]{3,2,1,0:T(8,128)S(1)}, u32[]{:S(2)}, u32[]{:S(2)}) collective-permute-start(f32[5,2,64,128]{3,2,1,0:T(8,128)S(1)} %get-tuple-element.28), channel_id=1, source_target_pairs={{2,0},{4,2},{6,4},{3,1},{5,3},{7,5},{10,8},{12,10},{14,12},{11,9},... | collective-permute-start | bytes 983048 | tf_op jit(solution)/shard_map/ppermute | solution.py:34
  73.9 5.9 %collective-permute-done.7 = f32[5,2,64,128]{3,2,1,0:T(8,128)S(1)} collective-permute-done((f32[5,2,64,128]{3,2,1,0:T(8,128)S(1)}, f32[5,2,64,128]{3,2,1,0:T(8,128)S(1)}, u32[]{:S(2)}, u32[]{:S(2)}) %collective-permute-start.7) | collective-permute-done | bytes 327712 | tf_op jit(solution)/shard_map/ppermute | solution.py:31
  79.8 7.8 %collective-permute-done.8 = f32[5,2,64,128]{3,2,1,0:T(8,128)S(1)} collective-permute-done((f32[5,2,64,128]{3,2,1,0:T(8,128)S(1)}, f32[5,2,64,128]{3,2,1,0:T(8,128)S(1)}, u32[]{:S(2)}, u32[]{:S(2)}) %collective-permute-start.8) | collective-permute-done | bytes 327712 | tf_op jit(solution)/shard_map/ppermute | solution.py:34
  87.7 1.6 %collective-permute-start.9 = (f32[5,8,2,128]{3,2,1,0:T(2,128)S(1)}, f32[5,8,2,128]{3,2,1,0:T(2,128)S(1)}, u32[]{:S(2)}, u32[]{:S(2)}) collective-permute-start(f32[5,8,2,128]{3,2,1,0:T(2,128)S(1)} %get-tuple-element.23), channel_id=1, source_target_pairs={{0,1},{2,3},{4,5},{6,7},{8,9},{10,11},{12,13},{14,15},{16,17},{18,... | collective-permute-start | bytes 122888 | tf_op jit(solution)/shard_map/ppermute | solution.py:31
  89.2 1.3 %collective-permute-start.10 = (f32[5,8,2,128]{3,2,1,0:T(2,128)S(1)}, f32[5,8,2,128]{3,2,1,0:T(2,128)S(1)}, u32[]{:S(2)}, u32[]{:S(2)}) collective-permute-start(f32[5,8,2,128]{3,2,1,0:T(2,128)S(1)} %get-tuple-element.24), channel_id=1, source_target_pairs={{1,0},{3,2},{5,4},{7,6},{9,8},{11,10},{13,12},{15,14},{17,16},{19,... | collective-permute-start | bytes 122888 | tf_op jit(solution)/shard_map/ppermute | solution.py:34
  90.7 1.7 %collective-permute-done.10 = f32[5,8,2,128]{3,2,1,0:T(2,128)S(1)} collective-permute-done((f32[5,8,2,128]{3,2,1,0:T(2,128)S(1)}, f32[5,8,2,128]{3,2,1,0:T(2,128)S(1)}, u32[]{:S(2)}, u32[]{:S(2)}) %collective-permute-start.10) | collective-permute-done | bytes 40992 | tf_op jit(solution)/shard_map/ppermute | solution.py:34
  93.3 1.0 %subtract_multiply_fusion = f32[2,8,65,128]{3,2,1,0:T(8,128)S(1)} fusion(f32[5,8,2,128]{3,2,1,0:T(2,128)S(1)} %collective-permute-done.10, f32[5,2,64,128]{3,2,1,0:T(8,128)S(1)} %collective-permute-done.8, f32[1,4,64,128]{3,2,1,0:T(8,128)S(1)} %bitcast.49, f32[1,4,64,128]{3,2,1,0:T(8,128)S(1)} %get-tuple-element.34, ...), kind=kLoop, calls=%fused_computation.29 | loop fusion | flops 6656000 | bytes 3056640 | tf_op jit(solution)/shard_map/mul | solution.py:65
  94.4 0.9 fusion.20
  (59 shorter events, 5.7 us)
Async XLA Ops:
  0.0 22.0 %copy-start.1 = (f32[2,2,1,8192]{3,2,1,0:T(1,128)S(1)}, f32[2,2,1,8192]{3,2,1,0:T(1,128)}, u32[]{:S(2)}) copy-start(f32[2,2,1,8192]{3,2,1,0:T(1,128)} %param.11) | copy-start | bytes 393220
  0.0 22.1 %copy-start.3 = (f32[4,64]{1,0:T(4,128)S(1)}, f32[4,64]{1,0:T(4,128)}, u32[]{:S(2)}) copy-start(f32[4,64]{1,0:T(4,128)} %param.10) | copy-start | bytes 3076
  0.0 22.4 %copy-start.2 = (f32[2,1,8192]{2,1,0:T(1,128)S(1)}, f32[2,1,8192]{2,1,0:T(1,128)}, u32[]{:S(2)}) copy-start(f32[2,1,8192]{2,1,0:T(1,128)} %param.12) | copy-start | bytes 196612
  0.0 38.9 %collective-permute-start.1 = (f32[2,2,1,8192]{3,2,1,0:T(1,128)}, f32[2,2,1,8192]{3,2,1,0:T(1,128)S(1)}, u32[]{:S(2)}, u32[]{:S(2)}) collective-permute-start(f32[2,2,1,8192]{3,2,1,0:T(1,128)} %param.11), channel_id=1, source_target_pairs={{0,24},{8,0},{16,8},{24,16},{1,25},{9,1},{17,9},{25,17},{2,26},{10... | collective-permute-start | bytes 393224 | tf_op jit(solution)/shard_map/ppermute | solution.py:19
  5.1 32.2 %collective-permute-start = (f32[2,2,1,8192]{3,2,1,0:T(1,128)}, f32[2,2,1,8192]{3,2,1,0:T(1,128)S(1)}, u32[]{:S(2)}, u32[]{:S(2)}) collective-permute-start(f32[2,2,1,8192]{3,2,1,0:T(1,128)} %param.11), channel_id=1, source_target_pairs={{0,8},{8,16},{16,24},{24,0},{1,9},{9,17},{17,25},{25,1},{2,10},{10... | collective-permute-start | bytes 393224 | tf_op jit(solution)/shard_map/ppermute | solution.py:16
  37.3 6.8 %collective-permute-start.2 = (f32[2,2,1,8192]{3,2,1,0:T(1,128)S(1)}, f32[2,2,1,8192]{3,2,1,0:T(1,128)S(1)}, u32[]{:S(2)}, u32[]{:S(2)}) collective-permute-start(f32[2,2,1,8192]{3,2,1,0:T(1,128)S(1)} %collective-permute-done), channel_id=1, source_target_pairs={{0,8},{8,16},{16,24},{24,0},{1,9},{9,17},{17,25},{25,1},{2,10},{10... | collective-permute-start | bytes 393224 | tf_op jit(solution)/shard_map/ppermute | solution.py:16
  44.8 8.7 %collective-permute-start.3 = (f32[6,2,64,128]{3,2,1,0:T(8,128)S(1)}, f32[6,2,64,128]{3,2,1,0:T(8,128)S(1)}, u32[]{:S(2)}, u32[]{:S(2)}) collective-permute-start(f32[6,2,64,128]{3,2,1,0:T(8,128)S(1)} %get-tuple-element.25), channel_id=1, source_target_pairs={{0,2},{2,4},{4,6},{1,3},{3,5},{5,7},{8,10},{10,12},{12,14},{9,11},... | collective-permute-start | bytes 1179656 | tf_op jit(solution)/shard_map/ppermute | solution.py:31
  48.2 12.8 %collective-permute-start.4 = (f32[6,2,64,128]{3,2,1,0:T(8,128)S(1)}, f32[6,2,64,128]{3,2,1,0:T(8,128)S(1)}, u32[]{:S(2)}, u32[]{:S(2)}) collective-permute-start(f32[6,2,64,128]{3,2,1,0:T(8,128)S(1)} %get-tuple-element.26), channel_id=1, source_target_pairs={{2,0},{4,2},{6,4},{3,1},{5,3},{7,5},{10,8},{12,10},{14,12},{11,9},... | collective-permute-start | bytes 1179656 | tf_op jit(solution)/shard_map/ppermute | solution.py:34
  61.1 2.6 %collective-permute-start.5 = (f32[6,8,2,128]{3,2,1,0:T(2,128)S(1)}, f32[6,8,2,128]{3,2,1,0:T(2,128)S(1)}, u32[]{:S(2)}, u32[]{:S(2)}) collective-permute-start(f32[6,8,2,128]{3,2,1,0:T(2,128)S(1)} %get-tuple-element.16), channel_id=1, source_target_pairs={{0,1},{2,3},{4,5},{6,7},{8,9},{10,11},{12,13},{14,15},{16,17},{18,... | collective-permute-start | bytes 147464 | tf_op jit(solution)/shard_map/ppermute | solution.py:31
  62.4 3.1 %collective-permute-start.6 = (f32[6,8,2,128]{3,2,1,0:T(2,128)S(1)}, f32[6,8,2,128]{3,2,1,0:T(2,128)S(1)}, u32[]{:S(2)}, u32[]{:S(2)}) collective-permute-start(f32[6,8,2,128]{3,2,1,0:T(2,128)S(1)} %get-tuple-element.17), channel_id=1, source_target_pairs={{1,0},{3,2},{5,4},{7,6},{9,8},{11,10},{13,12},{15,14},{17,16},{19,... | collective-permute-start | bytes 147464 | tf_op jit(solution)/shard_map/ppermute | solution.py:34
  67.8 1.0 %copy-start = (f32[2,4,64,128]{3,2,1,0:T(8,128)S(1)}, f32[2,4,64,128]{3,2,1,0:T(8,128)}, u32[]{:S(2)}) copy-start(f32[2,4,64,128]{3,2,1,0:T(8,128)} %param.7) | copy-start | bytes 786436
  69.2 10.7 %collective-permute-start.7 = (f32[5,2,64,128]{3,2,1,0:T(8,128)S(1)}, f32[5,2,64,128]{3,2,1,0:T(8,128)S(1)}, u32[]{:S(2)}, u32[]{:S(2)}) collective-permute-start(f32[5,2,64,128]{3,2,1,0:T(8,128)S(1)} %get-tuple-element.27), channel_id=1, source_target_pairs={{0,2},{2,4},{4,6},{1,3},{3,5},{5,7},{8,10},{10,12},{12,14},{9,11},... | collective-permute-start | bytes 983048 | tf_op jit(solution)/shard_map/ppermute | solution.py:31
  72.6 15.0 %collective-permute-start.8 = (f32[5,2,64,128]{3,2,1,0:T(8,128)S(1)}, f32[5,2,64,128]{3,2,1,0:T(8,128)S(1)}, u32[]{:S(2)}, u32[]{:S(2)}) collective-permute-start(f32[5,2,64,128]{3,2,1,0:T(8,128)S(1)} %get-tuple-element.28), channel_id=1, source_target_pairs={{2,0},{4,2},{6,4},{3,1},{5,3},{7,5},{10,8},{12,10},{14,12},{11,9},... | collective-permute-start | bytes 983048 | tf_op jit(solution)/shard_map/ppermute | solution.py:34
  87.7 3.0 %collective-permute-start.9 = (f32[5,8,2,128]{3,2,1,0:T(2,128)S(1)}, f32[5,8,2,128]{3,2,1,0:T(2,128)S(1)}, u32[]{:S(2)}, u32[]{:S(2)}) collective-permute-start(f32[5,8,2,128]{3,2,1,0:T(2,128)S(1)} %get-tuple-element.23), channel_id=1, source_target_pairs={{0,1},{2,3},{4,5},{6,7},{8,9},{10,11},{12,13},{14,15},{16,17},{18,... | collective-permute-start | bytes 122888 | tf_op jit(solution)/shard_map/ppermute | solution.py:31
  89.2 3.1 %collective-permute-start.10 = (f32[5,8,2,128]{3,2,1,0:T(2,128)S(1)}, f32[5,8,2,128]{3,2,1,0:T(2,128)S(1)}, u32[]{:S(2)}, u32[]{:S(2)}) collective-permute-start(f32[5,8,2,128]{3,2,1,0:T(2,128)S(1)} %get-tuple-element.24), channel_id=1, source_target_pairs={{1,0},{3,2},{5,4},{7,6},{9,8},{11,10},{13,12},{15,14},{17,16},{19,... | collective-permute-start | bytes 122888 | tf_op jit(solution)/shard_map/ppermute | solution.py:34
